TPU v7x, 32 devices: a whole 2x2x4 slice. The times are simulated.
32 devices in a mesh: row: 4 (over y, x), col: 8 (over z, core).
Axes of the slice: x: 2, y: 2, z: 4, core: 2. Of those that a mesh axis runs over, the one named last changes fastest.
Arguments:
- pair_repr: bfloat16 [1024, 1024, 128], P('row', 'col'), may hold values from -6 to 6
- logit_cotangent: bfloat16 [1024, 1024, 128], P('row', 'col'), may hold values from -6 to 6
- pair_mask: int32 [1024, 1024], P('row', 'col'), may hold values 0 or 1
- single_repr: bfloat16 [1024, 384], P(('row', 'col')), may hold values from -6 to 6
- token_index: int32 [1024], replicated, may hold values from 0 to 2046, as said below
- pair_up: bfloat16 [128, 512], replicated, may hold values from -0.5 to 0.5
- pair_gate: bfloat16 [128, 512], replicated, may hold values from -0.5 to 0.5
- pair_down: bfloat16 [512, 128], replicated, may hold values from -0.25 to 0.25
- head_weight: bfloat16 [128, 128], replicated, may hold values from -0.5 to 0.5
- rel_table: bfloat16 [65, 128], replicated, may hold values from -3 to 3
- proj_row: bfloat16 [384, 128], replicated, may hold values from -0.3125 to 0.3125
- proj_col: bfloat16 [384, 128], replicated, may hold values from -0.3125 to 0.3125
- single_gate: bfloat16 [384, 1536], replicated, may hold values from -0.3125 to 0.3125
- single_up: bfloat16 [384, 1536], replicated, may hold values from -0.3125 to 0.3125
- single_down: bfloat16 [1536, 384], replicated, may hold values from -0.15625 to 0.15625
Outputs:
- pair_grad: bfloat16 [1024, 1024, 128], P('row', 'col')
- single_grad: bfloat16 [1024, 384], P(('row', 'col'))
- grad_pair_up: float32 [128, 512], replicated
- grad_pair_gate: float32 [128, 512], replicated
- grad_pair_down: float32 [512, 128], replicated
- grad_head: float32 [128, 128], replicated
- grad_rel: float32 [65, 128], replicated
- grad_proj_row: float32 [384, 128], replicated
- grad_proj_col: float32 [384, 128], replicated
- grad_single_gate: float32 [384, 1536], P(None, ('row', 'col'))
- grad_single_up: float32 [384, 1536], P(None, ('row', 'col'))
- grad_single_down: float32 [1536, 384], P(('row', 'col'))
Inputs may be any that keep to these rules, and one draw needn't show every extreme that they name: `token_index`: strictly increasing, entry 0 is 0, successive entries differ by 1 to 3, the last entry is 2046.
All inputs are finite; a program needn't handle non-finite values. No bound on the sum of `pair_mask` on one device may be relied on, other than what follows from the above.
Results may differ from a plain program's by a relative error of at most 0.018.
Values may be sent and summed in bfloat16 or wider, within the bound.
No kernel may reach another device: no remote copies, remote signals or barrier semaphores. Data moves between devices by JAX's collectives and lax.ppermute only.
A program may use at most 192 MiB of HBM per device.

v0:
```python
import jax
import jax.numpy as jnp
from jax import lax
from jax.sharding import PartitionSpec as P

norm_eps = 1e-05


def gated_parts(gate):
    sigma = jax.nn.sigmoid(gate)
    return (gate * sigma, sigma * (1.0 + gate * (1.0 - sigma)))


def product(matrix_a, matrix_b):
    return jnp.dot(matrix_a, matrix_b, preferred_element_type=jnp.float32)


def product_left(matrix_a, matrix_b):
    return lax.dot_general(
        matrix_a, matrix_b, (((0,), (0,)), ((), ())), preferred_element_type=jnp.float32
    )


def product_right(matrix_a, matrix_b):
    return lax.dot_general(
        matrix_a, matrix_b, (((1,), (1,)), ((), ())), preferred_element_type=jnp.float32
    )


def single_forward(single_repr, single_gate, single_up, single_down):
    source = single_repr.astype(jnp.float32)
    inverse_rms = lax.rsqrt(jnp.mean(source * source, axis=-1, keepdims=True) + norm_eps)
    normed = source * inverse_rms
    normed_bf = normed.astype(jnp.bfloat16)
    gate_pre = product(normed_bf, single_gate)
    up_pre = product(normed_bf, single_up)
    silu_value, silu_slope = gated_parts(gate_pre)
    hidden = (silu_value * up_pre).astype(jnp.bfloat16)
    updated = (source + product(hidden, single_down)).astype(jnp.bfloat16)
    return (normed, inverse_rms, normed_bf, up_pre, silu_value, silu_slope, hidden, updated)


def single_backward(grad_in, saved_state, single_gate, single_up, single_down):
    normed, inverse_rms, normed_bf, up_pre, silu_value, silu_slope, hidden, updated = saved_state
    grad_bf = grad_in.astype(jnp.bfloat16)
    grad_hidden = product_right(grad_bf, single_down)
    grad_up = (grad_hidden * silu_value).astype(jnp.bfloat16)
    grad_gate = (grad_hidden * up_pre * silu_slope).astype(jnp.bfloat16)
    grad_normed = product_right(grad_gate, single_gate) + product_right(grad_up, single_up)
    grad_source = grad_in + inverse_rms * (
        grad_normed - normed * jnp.mean(grad_normed * normed, axis=-1, keepdims=True)
    )
    return (grad_source, grad_bf, grad_gate, grad_up)


def local_weight_sums(normed_bf, grad_bf, grad_gate, grad_up, hidden):
    return jnp.stack(
        [
            product_left(normed_bf, grad_gate),
            product_left(normed_bf, grad_up),
            product_left(grad_bf, hidden),
        ],
        axis=0,
    )


def pair_block(
    pair_blk,
    cot_blk,
    mirror_blk,
    row_blk,
    col_blk,
    row_pos,
    col_pos,
    rel_table,
    up_gate,
    pair_down,
    head_weight,
):
    n_rows, n_cols, pair_width = pair_blk.shape
    bin_count = mirror_blk.shape[2]
    rel_count = rel_table.shape[0]
    rel_span = (rel_count - 1) // 2
    pair_count = n_rows * n_cols
    offset = jnp.clip(row_pos[:, None] - col_pos[None, :], -rel_span, rel_span) + rel_span
    one_hot = offset.reshape(pair_count, 1) == jnp.arange(rel_count, dtype=jnp.int32)[None, :]
    hot_table = one_hot.astype(jnp.bfloat16)
    pair_in = (
        pair_blk.astype(jnp.float32)
        + row_blk.astype(jnp.float32)[:, None, :]
        + col_blk.astype(jnp.float32)[None, :, :]
    )
    pair_in = pair_in.reshape(pair_count, pair_width) + product(hot_table, rel_table)
    centred = pair_in - jnp.mean(pair_in, axis=-1, keepdims=True)
    inv_std = lax.rsqrt(jnp.mean(centred * centred, axis=-1, keepdims=True) + norm_eps)
    normed = centred * inv_std
    normed_bf = normed.astype(jnp.bfloat16)
    hidden_width = up_gate.shape[1] // 2
    both_pre = product(normed_bf, up_gate)
    up_pre = both_pre[:, :hidden_width]
    gate_pre = both_pre[:, hidden_width:]
    silu_value, silu_slope = gated_parts(gate_pre)
    hidden = (silu_value * up_pre).astype(jnp.bfloat16)
    pair_out = (pair_in + product(hidden, pair_down)).astype(jnp.bfloat16)
    cot_flat = cot_blk.reshape(pair_count, 2 * bin_count)
    symmetric = (
        cot_flat[:, bin_count:].astype(jnp.float32)
        + mirror_blk.reshape(pair_count, bin_count).astype(jnp.float32)
    ).astype(jnp.bfloat16)
    head_cot = jnp.concatenate([cot_flat[:, :bin_count], symmetric], axis=1)
    grad_out = product_right(head_cot, head_weight)
    grad_out_bf = grad_out.astype(jnp.bfloat16)
    grad_hidden = product_right(grad_out_bf, pair_down)
    grad_both = jnp.concatenate(
        [
            (grad_hidden * silu_value).astype(jnp.bfloat16),
            (grad_hidden * up_pre * silu_slope).astype(jnp.bfloat16),
        ],
        axis=1,
    )
    grad_normed = product_right(grad_both, up_gate)
    grad_in = grad_out + inv_std * (
        grad_normed
        - jnp.mean(grad_normed, axis=-1, keepdims=True)
        - normed * jnp.mean(grad_normed * normed, axis=-1, keepdims=True)
    )
    head_sum = product_left(pair_out, head_cot)
    down_sum = product_left(hidden, grad_out_bf)
    up_gate_sum = product_left(normed_bf, grad_both)
    rel_sum = lax.dot_general(
        one_hot.astype(jnp.float32),
        grad_in,
        (((0,), (0,)), ((), ())),
        precision=lax.Precision.HIGHEST,
        preferred_element_type=jnp.float32,
    )
    grad_tile = grad_in.reshape(n_rows, n_cols, pair_width)
    return (
        grad_tile.astype(jnp.bfloat16),
        jnp.sum(grad_tile, axis=1),
        jnp.sum(grad_tile, axis=0),
        up_gate_sum,
        down_sum,
        head_sum,
        rel_sum,
    )


def local(
    pair_repr,
    logit_cotangent,
    pair_mask,
    single_repr,
    token_index,
    pair_up,
    pair_gate,
    pair_down,
    head_weight,
    rel_table,
    proj_row,
    proj_col,
    single_gate,
    single_up,
    single_down,
):
    n_row = lax.axis_size("row")
    n_col = lax.axis_size("col")
    row_index = lax.axis_index("row")
    col_index = lax.axis_index("col")
    joint_index = row_index * n_col + col_index
    tile_rows, tile_cols, pair_width = pair_repr.shape
    bin_count = logit_cotangent.shape[2] // 2
    strip_len = single_repr.shape[0]
    tokens_all = strip_len * n_row * n_col
    hidden_width = pair_up.shape[1]
    saved_state = single_forward(single_repr, single_gate, single_up, single_down)
    updated = saved_state[7]
    row_piece = product(updated, proj_row).astype(jnp.bfloat16)
    col_piece = product(updated, proj_col).astype(jnp.bfloat16)
    row_proj = lax.all_gather(row_piece, "col", axis=0, tiled=True)
    col_whole = lax.all_gather(col_piece, ("row", "col"), axis=0, tiled=True)
    col_proj = lax.dynamic_slice_in_dim(col_whole, col_index * tile_cols, tile_cols, 0)
    masked = logit_cotangent * pair_mask[:, :, None].astype(jnp.bfloat16)
    distance_part = masked[:, :, bin_count:].reshape(tile_rows, tile_cols * bin_count)
    strips = lax.all_to_all(distance_part, "col", split_axis=0, concat_axis=1, tiled=True)
    columns = lax.all_to_all(strips, ("row", "col"), split_axis=1, concat_axis=0, tiled=True)
    returned = lax.all_to_all(columns, "col", split_axis=0, concat_axis=1, tiled=True)
    mirrored = returned.reshape(tile_cols, tile_rows, bin_count).transpose(1, 0, 2)
    up_gate = jnp.concatenate([pair_up, pair_gate], axis=1)
    row_pos = lax.dynamic_slice_in_dim(token_index, row_index * tile_rows, tile_rows, 0)
    col_pos = lax.dynamic_slice_in_dim(token_index, col_index * tile_cols, tile_cols, 0)
    block_count = 4
    block_rows = tile_rows // block_count

    def block_step(running, inputs):
        pair_blk, cot_blk, mirror_blk, row_blk, pos_blk = inputs
        grad_blk, row_sum, col_sum, up_gate_sum, down_sum, head_sum, rel_sum = pair_block(
            pair_blk,
            cot_blk,
            mirror_blk,
            row_blk,
            col_proj,
            pos_blk,
            col_pos,
            rel_table,
            up_gate,
            pair_down,
            head_weight,
        )
        running = (
            running[0] + col_sum,
            running[1] + up_gate_sum,
            running[2] + down_sum,
            running[3] + head_sum,
            running[4] + rel_sum,
        )
        return (running, (grad_blk, row_sum))

    initial = (
        jnp.zeros((tile_cols, pair_width), jnp.float32),
        jnp.zeros(up_gate.shape, jnp.float32),
        jnp.zeros(pair_down.shape, jnp.float32),
        jnp.zeros(head_weight.shape, jnp.float32),
        jnp.zeros(rel_table.shape, jnp.float32),
    )
    sliced = (
        pair_repr.reshape(block_count, block_rows, tile_cols, pair_width),
        masked.reshape(block_count, block_rows, tile_cols, 2 * bin_count),
        mirrored.reshape(block_count, block_rows, tile_cols, bin_count),
        row_proj.reshape(block_count, block_rows, pair_width),
        row_pos.reshape(block_count, block_rows),
    )
    sums_out, blocks_out = lax.scan(block_step, initial, sliced)
    col_total, up_gate_sum, down_sum, head_sum, rel_sum = sums_out
    grad_blocks, row_sums = blocks_out
    pair_grad = grad_blocks.reshape(tile_rows, tile_cols, pair_width)
    row_tile = row_sums.reshape(tile_rows, pair_width)
    row_part = lax.psum_scatter(
        row_tile.astype(jnp.bfloat16), "col", scatter_dimension=0, tiled=True
    )
    col_summed = lax.psum(col_total.astype(jnp.bfloat16), "row")
    col_every = lax.all_gather(col_summed, "col", axis=0, tiled=True)
    col_bf = lax.dynamic_slice_in_dim(col_every, joint_index * strip_len, strip_len, 0)
    single_cot = product_right(row_part, proj_row) + product_right(col_bf, proj_col)
    prow_sum = product_left(updated, row_part)
    pcol_sum = product_left(updated, col_bf)
    grad_source, grad_bf, grad_gate, grad_up = single_backward(
        single_cot, saved_state, single_gate, single_up, single_down
    )
    normed_bf = saved_state[2]
    hidden = saved_state[6]
    stacked = local_weight_sums(normed_bf, grad_bf, grad_gate, grad_up, hidden)
    summed = lax.psum(stacked, ("row", "col"))
    share_len = summed.shape[2] // (n_row * n_col)
    own_share = lax.dynamic_slice_in_dim(summed, joint_index * share_len, share_len, 2)
    totals = lax.psum(
        (up_gate_sum, down_sum, head_sum, rel_sum, prow_sum, pcol_sum), ("row", "col")
    )
    grad_scale = 1.0 / tokens_all
    return (
        pair_grad,
        grad_source.astype(jnp.bfloat16),
        totals[0][:, :hidden_width] * grad_scale,
        totals[0][:, hidden_width:] * grad_scale,
        totals[1] * grad_scale,
        totals[2] * grad_scale,
        totals[3] * grad_scale,
        totals[4] * grad_scale,
        totals[5] * grad_scale,
        own_share[0] * grad_scale,
        own_share[1] * grad_scale,
        jnp.transpose(own_share[2]) * grad_scale,
    )


def solution(mesh):
    placed = (
        P("row", "col", None),
        P("row", "col", None),
        P("row", "col"),
        P(("row", "col"), None),
        P(),
        P(),
        P(),
        P(),
        P(),
        P(),
        P(),
        P(),
        P(),
        P(),
        P(),
    )
    return jax.shard_map(
        local,
        mesh=mesh,
        in_specs=placed,
        out_specs=(
            P("row", "col", None),
            P(("row", "col"), None),
            P(),
            P(),
            P(),
            P(),
            P(),
            P(),
            P(),
            P(None, ("row", "col")),
            P(None, ("row", "col")),
            P(("row", "col"), None),
        ),
        check_vma=False,
    )
```

profile of v0, /device:TPU:0, one launch (start us, length us, event | category | flops | bytes accessed | tf_op | source)
XLA Modules:
  0.0 1154.7 jit_solution(11379093476381169805)
XLA Ops:
  8.2 8.6 broadcast_multiply_fusion.3
  16.8 9.9 slice.44
  26.8 12.1 %all_to_all.36 = bf16[8,32,8192]{2,1,0:T(8,128)(2,1)} reshape(bf16[256,128,64]{2,1,0:T(8,128)(2,1)} %slice.44) | data formatting | bytes 8388608 | tf_op jit(solution)/shard_map/all_to_all | solution.py:185
  38.8 100.3 %all_to_all.48 = bf16[8,32,8192]{2,1,0:T(8,128)(2,1)S(1)} all-to-all(bf16[8,32,8192]{2,1,0:T(8,128)(2,1)} %all_to_all.36), channel_id=1, replica_groups=mesh['row'=4,'col'=8] {'col'}, dimensions={0} | all-to-all | bytes 8388608 | tf_op jit(solution)/shard_map/all_to_all | solution.py:185
  139.1 4.3 copy.44
  143.4 7.9 all_to_all.39
  151.4 4.5 copy.45
  155.8 98.3 %all_to_all.49 = bf16[32,32,2048]{2,0,1:T(8,128)(2,1)} all-to-all(bf16[32,32,2048]{2,0,1:T(8,128)(2,1)S(1)} %copy.45), channel_id=1, replica_groups=mesh['row'=4,'col'=8] {'row','col'}, dimensions={1} | all-to-all | bytes 8388608 | tf_op jit(solution)/shard_map/all_to_all | solution.py:186
  254.2 4.7 all-to-all-start.2
  265.2 94.8 %all_gather.9 = bf16[256,128]{1,0:T(8,128)(2,1)} all-gather(bf16[32,128]{1,0:T(8,128)(2,1)S(1)} %convolution_convert_fusion.1), channel_id=1, replica_groups=mesh['row'=4,'col'=8] {'col'}, dimensions={0}, use_global_device_ids=true | all-gather | bytes 73728 | tf_op jit(solution)/shard_map/all_gather | solution.py:180
  360.1 40.0 %all_gather.10 = bf16[1024,128]{1,0:T(8,128)(2,1)S(1)} all-gather(bf16[32,128]{1,0:T(8,128)(2,1)S(1)} %convolution_convert_fusion), channel_id=1, replica_groups=mesh['row'=4,'col'=8] {'row','col'}, dimensions={0}, use_global_device_ids=true | all-gather | bytes 270336 | tf_op jit(solution)/shard_map/all_gather | solution.py:181
  400.9 6.5 copy.46
  407.4 482.4 %while.23 = (s32[]{:T(128)}, f32[128,128]{1,0:T(8,128)}, f32[128,1024]{1,0:T(8,128)}, f32[512,128]{1,0:T(8,128)}, f32[128,128]{1,0:T(8,128)}, /*index=5*/f32[65,...) while((s32[]{:T(128)}, f32[128,128]{1,0:T(8,128)}, ...), condition=%wide.region_8.9_spmd.clone, body=%wide.region_1.8_spmd.clone.sunk | while | flops 11331420160 | bytes 375022848 | solution.py:233
  423.4 2.5 constant_dynamic-slice_fusion.7
  433.8 12.2 %fusion.127 = f32[8192,1024]{0,1:T(8,128)} fusion(bf16[128,1024]{1,0:T(8,128)(2,1)S(1)} %copy-done.9, f32[8192,128]{1,0:T(8,128)S(1)} %get-tuple-element.485, f32[8192]{0:T(1024)S(1)} %add_rsqrt_fusion.3, f32[8192]{0:T(1024)S(1)} %broadcast_multiply_fusion.13), kind=kOutput, calls=%fused_computation.53.clone.1 | convolution fusion | flops 2150629376 | bytes 38076416 | tf_op jit(solution)/shard_map/while/body/eval_jaxpr/dot_general | solution.py:15
  448.3 2.7 copy.53
  453.4 3.2 fusion.124
  456.7 22.8 %multiply_convert_fusion.7 = (bf16[8192,512]{0,1:T(8,128)(2,1)}, bf16[8192,512]{0,1:T(8,128)(2,1)}, bf16[8192,512]{0,1:T(8,128)(2,1)}) fusion(f32[8192,1024]{0,1:T(8,128)} %fusion.127, bf16[512,128]{1,0:T(8,128)(2,1)S(1)} %get-tuple-element.556, f32[8192,128]{1,0:T(8,128)} %fusion.124), kind=kOutput, calls=%fused_computation.3.clone.1 | convolution fusion | flops 1137704960 | bytes 63045632 | tf_op jit(solution)/shard_map/while/body/eval_jaxpr/dot_general | solution.py:25
  479.4 13.2 %fusion.128 = (f32[8192]{0:T(1024)S(1)}, f32[8192]{0:T(1024)S(1)}, f32[8192,128]{1,0:T(8,128)S(1)}) fusion(f32[8192]{0:T(1024)S(1)} %add_rsqrt_fusion.3, f32[8192,128]{1,0:T(8,128)S(1)} %copy-done.2, f32[8192]{0:T(1024)S(1)} %broadcast_multiply_fusion.13, bf16[128,1024]{1,0:T(8,128)(2,1)S(1)} %copy-done.10, ...), kind=kOutput, calls=%fused_computation.108.clone.1 | convolution fusion | flops 2186264576 | bytes 25559040 | tf_op jit(solution)/shard_map/while/body/eval_jaxpr/dot_general | solution.py:25
  492.7 5.0 bitcast_reduce_fusion.2
  500.8 11.2 fusion.130
  512.1 7.8 convolution_add_fusion.7
  519.9 12.5 %fusion.129 = f32[128,1024]{1,0:T(8,128)S(1)} fusion(bf16[8192,512]{0,1:T(8,128)(2,1)} %get-tuple-element.487, bf16[8192,512]{0,1:T(8,128)(2,1)} %get-tuple-element.488, f32[128,1024]{1,0:T(8,128)S(1)} %copy-done.26, pred[]{:T(512)S(6)} %compare.3, f32[8192,128]{1,0:T(8,128)S(1)} %copy-done.3, f32[8192]{0:T(1024)S(1)} %add_rsqrt_fusion.3, ...), kind=kOutput, calls=%fused_computation.23.clone.1 | convolution fusion | flops 2184445952 | bytes 22085632 | tf_op jit(solution)/shard_map/while/body/eval_jaxpr/dot_general | solution.py:19
  532.5 2.6 reduce_sum.96
  535.1 4.2 fusion.131
  550.4 12.2 %fusion.127 = f32[8192,1024]{0,1:T(8,128)} fusion(bf16[128,1024]{1,0:T(8,128)(2,1)S(1)} %copy-done.9, f32[8192,128]{1,0:T(8,128)S(1)} %get-tuple-element.485, f32[8192]{0:T(1024)S(1)} %add_rsqrt_fusion.3, f32[8192]{0:T(1024)S(1)} %broadcast_multiply_fusion.13), kind=kOutput, calls=%fused_computation.53.clone.1 | convolution fusion | flops 2150629376 | bytes 38076416 | tf_op jit(solution)/shard_map/while/body/eval_jaxpr/dot_general | solution.py:15
  564.8 2.7 copy.53
  570.0 3.2 fusion.124
  573.2 22.8 %multiply_convert_fusion.7 = (bf16[8192,512]{0,1:T(8,128)(2,1)}, bf16[8192,512]{0,1:T(8,128)(2,1)}, bf16[8192,512]{0,1:T(8,128)(2,1)}) fusion(f32[8192,1024]{0,1:T(8,128)} %fusion.127, bf16[512,128]{1,0:T(8,128)(2,1)S(1)} %get-tuple-element.556, f32[8192,128]{1,0:T(8,128)} %fusion.124), kind=kOutput, calls=%fused_computation.3.clone.1 | convolution fusion | flops 1137704960 | bytes 63045632 | tf_op jit(solution)/shard_map/while/body/eval_jaxpr/dot_general | solution.py:25
  596.0 13.2 %fusion.128 = (f32[8192]{0:T(1024)S(1)}, f32[8192]{0:T(1024)S(1)}, f32[8192,128]{1,0:T(8,128)S(1)}) fusion(f32[8192]{0:T(1024)S(1)} %add_rsqrt_fusion.3, f32[8192,128]{1,0:T(8,128)S(1)} %copy-done.2, f32[8192]{0:T(1024)S(1)} %broadcast_multiply_fusion.13, bf16[128,1024]{1,0:T(8,128)(2,1)S(1)} %copy-done.10, ...), kind=kOutput, calls=%fused_computation.108.clone.1 | convolution fusion | flops 2186264576 | bytes 25559040 | tf_op jit(solution)/shard_map/while/body/eval_jaxpr/dot_general | solution.py:25
  609.3 5.0 bitcast_reduce_fusion.2
  617.4 11.2 fusion.130
  628.6 7.8 convolution_add_fusion.7
  636.4 12.5 %fusion.129 = f32[128,1024]{1,0:T(8,128)S(1)} fusion(bf16[8192,512]{0,1:T(8,128)(2,1)} %get-tuple-element.487, bf16[8192,512]{0,1:T(8,128)(2,1)} %get-tuple-element.488, f32[128,1024]{1,0:T(8,128)S(1)} %copy-done.26, pred[]{:T(512)S(6)} %compare.3, f32[8192,128]{1,0:T(8,128)S(1)} %copy-done.3, f32[8192]{0:T(1024)S(1)} %add_rsqrt_fusion.3, ...), kind=kOutput, calls=%fused_computation.23.clone.1 | convolution fusion | flops 2184445952 | bytes 22085632 | tf_op jit(solution)/shard_map/while/body/eval_jaxpr/dot_general | solution.py:19
  649.0 2.6 reduce_sum.96
  651.7 4.2 fusion.131
  666.9 12.2 %fusion.127 = f32[8192,1024]{0,1:T(8,128)} fusion(bf16[128,1024]{1,0:T(8,128)(2,1)S(1)} %copy-done.9, f32[8192,128]{1,0:T(8,128)S(1)} %get-tuple-element.485, f32[8192]{0:T(1024)S(1)} %add_rsqrt_fusion.3, f32[8192]{0:T(1024)S(1)} %broadcast_multiply_fusion.13), kind=kOutput, calls=%fused_computation.53.clone.1 | convolution fusion | flops 2150629376 | bytes 38076416 | tf_op jit(solution)/shard_map/while/body/eval_jaxpr/dot_general | solution.py:15
  681.4 2.7 copy.53
  686.5 3.2 fusion.124
  689.8 22.8 %multiply_convert_fusion.7 = (bf16[8192,512]{0,1:T(8,128)(2,1)}, bf16[8192,512]{0,1:T(8,128)(2,1)}, bf16[8192,512]{0,1:T(8,128)(2,1)}) fusion(f32[8192,1024]{0,1:T(8,128)} %fusion.127, bf16[512,128]{1,0:T(8,128)(2,1)S(1)} %get-tuple-element.556, f32[8192,128]{1,0:T(8,128)} %fusion.124), kind=kOutput, calls=%fused_computation.3.clone.1 | convolution fusion | flops 1137704960 | bytes 63045632 | tf_op jit(solution)/shard_map/while/body/eval_jaxpr/dot_general | solution.py:25
  712.5 13.2 %fusion.128 = (f32[8192]{0:T(1024)S(1)}, f32[8192]{0:T(1024)S(1)}, f32[8192,128]{1,0:T(8,128)S(1)}) fusion(f32[8192]{0:T(1024)S(1)} %add_rsqrt_fusion.3, f32[8192,128]{1,0:T(8,128)S(1)} %copy-done.2, f32[8192]{0:T(1024)S(1)} %broadcast_multiply_fusion.13, bf16[128,1024]{1,0:T(8,128)(2,1)S(1)} %copy-done.10, ...), kind=kOutput, calls=%fused_computation.108.clone.1 | convolution fusion | flops 2186264576 | bytes 25559040 | tf_op jit(solution)/shard_map/while/body/eval_jaxpr/dot_general | solution.py:25
  725.8 5.0 bitcast_reduce_fusion.2
  733.9 11.2 fusion.130
  745.2 7.8 convolution_add_fusion.7
  753.0 12.5 %fusion.129 = f32[128,1024]{1,0:T(8,128)S(1)} fusion(bf16[8192,512]{0,1:T(8,128)(2,1)} %get-tuple-element.487, bf16[8192,512]{0,1:T(8,128)(2,1)} %get-tuple-element.488, f32[128,1024]{1,0:T(8,128)S(1)} %copy-done.26, pred[]{:T(512)S(6)} %compare.3, f32[8192,128]{1,0:T(8,128)S(1)} %copy-done.3, f32[8192]{0:T(1024)S(1)} %add_rsqrt_fusion.3, ...), kind=kOutput, calls=%fused_computation.23.clone.1 | convolution fusion | flops 2184445952 | bytes 22085632 | tf_op jit(solution)/shard_map/while/body/eval_jaxpr/dot_general | solution.py:19
  765.5 2.6 reduce_sum.96
  768.2 4.2 fusion.131
  783.5 12.2 %fusion.127 = f32[8192,1024]{0,1:T(8,128)} fusion(bf16[128,1024]{1,0:T(8,128)(2,1)S(1)} %copy-done.9, f32[8192,128]{1,0:T(8,128)S(1)} %get-tuple-element.485, f32[8192]{0:T(1024)S(1)} %add_rsqrt_fusion.3, f32[8192]{0:T(1024)S(1)} %broadcast_multiply_fusion.13), kind=kOutput, calls=%fused_computation.53.clone.1 | convolution fusion | flops 2150629376 | bytes 38076416 | tf_op jit(solution)/shard_map/while/body/eval_jaxpr/dot_general | solution.py:15
  797.9 2.7 copy.53
  803.1 3.2 fusion.124
  806.3 22.8 %multiply_convert_fusion.7 = (bf16[8192,512]{0,1:T(8,128)(2,1)}, bf16[8192,512]{0,1:T(8,128)(2,1)}, bf16[8192,512]{0,1:T(8,128)(2,1)}) fusion(f32[8192,1024]{0,1:T(8,128)} %fusion.127, bf16[512,128]{1,0:T(8,128)(2,1)S(1)} %get-tuple-element.556, f32[8192,128]{1,0:T(8,128)} %fusion.124), kind=kOutput, calls=%fused_computation.3.clone.1 | convolution fusion | flops 1137704960 | bytes 63045632 | tf_op jit(solution)/shard_map/while/body/eval_jaxpr/dot_general | solution.py:25
  829.1 13.2 %fusion.128 = (f32[8192]{0:T(1024)S(1)}, f32[8192]{0:T(1024)S(1)}, f32[8192,128]{1,0:T(8,128)S(1)}) fusion(f32[8192]{0:T(1024)S(1)} %add_rsqrt_fusion.3, f32[8192,128]{1,0:T(8,128)S(1)} %copy-done.2, f32[8192]{0:T(1024)S(1)} %broadcast_multiply_fusion.13, bf16[128,1024]{1,0:T(8,128)(2,1)S(1)} %copy-done.10, ...), kind=kOutput, calls=%fused_computation.108.clone.1 | convolution fusion | flops 2186264576 | bytes 25559040 | tf_op jit(solution)/shard_map/while/body/eval_jaxpr/dot_general | solution.py:25
  842.3 5.0 bitcast_reduce_fusion.2
  850.5 11.2 fusion.130
  861.7 7.8 convolution_add_fusion.7
  869.5 12.5 %fusion.129 = f32[128,1024]{1,0:T(8,128)S(1)} fusion(bf16[8192,512]{0,1:T(8,128)(2,1)} %get-tuple-element.487, bf16[8192,512]{0,1:T(8,128)(2,1)} %get-tuple-element.488, f32[128,1024]{1,0:T(8,128)S(1)} %copy-done.26, pred[]{:T(512)S(6)} %compare.3, f32[8192,128]{1,0:T(8,128)S(1)} %copy-done.3, f32[8192]{0:T(1024)S(1)} %add_rsqrt_fusion.3, ...), kind=kOutput, calls=%fused_computation.23.clone.1 | convolution fusion | flops 2184445952 | bytes 22085632 | tf_op jit(solution)/shard_map/while/body/eval_jaxpr/dot_general | solution.py:19
  882.1 2.6 reduce_sum.96
  884.8 4.2 fusion.131
  890.7 14.0 %psum.56 = bf16[128,128]{1,0:T(8,128)(2,1)S(1)} all-reduce(bf16[128,128]{1,0:T(8,128)(2,1)S(1)} %convert_element_type.121), channel_id=1, replica_groups=mesh['row'=4,'col'=8] {'row'}, use_global_device_ids=true, to_apply=%region_10.11 | all-reduce | flops 16384 | bytes 65536 | tf_op jit(solution)/shard_map/psum | solution.py:241
  904.6 14.2 %all_gather.11 = bf16[1024,128]{1,0:T(8,128)(2,1)S(1)} all-gather(bf16[128,128]{1,0:T(8,128)(2,1)S(1)} %psum.56), channel_id=1, replica_groups=mesh['row'=4,'col'=8] {'col'}, dimensions={0}, use_global_device_ids=true | all-gather | bytes 294912 | tf_op jit(solution)/shard_map/all_gather | solution.py:242
  920.5 26.6 %reduce-scatter.2.cloned.1.call-done = bf16[32,128]{1,0:T(8,128)(2,1)} async-done(((bf16[256,128]{1,0:T(8,128)(2,1)}), bf16[32,128]{1,0:T(8,128)(2,1)}) %reduce-scatter.2.cloned.1.call-update) | async-done | bytes 8208 | tf_op jit(solution)/shard_map/reduce_scatter | solution.py:238
  953.7 3.4 pad_maximum_fusion.8
  958.8 40.0 %psum.60 = f32[65,128]{1,0:T(8,128)S(1)} all-reduce(f32[65,128]{1,0:T(8,128)S(1)} %copy-done.20), channel_id=1, replica_groups=mesh['row'=4,'col'=8] {'row','col'}, use_global_device_ids=true, to_apply=%region_15.16 | all-reduce | flops 8320 | bytes 66560 | tf_op jit(solution)/shard_map/psum | solution.py:256
  1001.2 135.8 %all-reduce.3.cloned.1.call-done = (f32[128,1024]{1,0:T(8,128)}, f32[512,128]{1,0:T(8,128)}, f32[128,128]{1,0:T(8,128)}, f32[384,128]{1,0:T(8,128)}, f32[384,128]{1,0:T(8,128)}, /*index=5*/f32[3,384,1536]{2,1,0:T(8,128)}) async-done(((f32[128,1024]{1,0:T(8,128)}, f32[512,128]{1,0:T(8,128)}, f32[128,128]{1,0:T(8,128)}, f32[384,128]{1,0:T(8,128)}, f32[384,128]{1,0:T(8,128)}, ...) | async-done | bytes 8323088 | tf_op jit(solution)/shard_map/psum | solution.py:256
  (298 shorter events, 104.1 us)
Async XLA Ops:
  7.2 255.2 %copy-start = (bf16[384,1536]{1,0:T(8,128)(2,1)S(1)}, bf16[384,1536]{1,0:T(8,128)(2,1)}, u32[]{:S(2)}) copy-start(bf16[384,1536]{1,0:T(8,128)(2,1)} %param.30) | copy-start | bytes 3538948
  254.2 7.7 copy-start.16
  254.2 7.8 copy-start.11
  254.2 146.7 %all-to-all-start.2 = ((bf16[8,128,2048]{2,1,0:T(8,128)(2,1)}), bf16[8,128,2048]{2,1,0:T(8,128)(2,1)}, u32[]{:S(2)}, u32[]{:S(2)}) async-start(bf16[8,128,2048]{2,1,0:T(8,128)(2,1)} %bitcast.135), calls=%async_computation.2 | async-start | bytes 8388608 | tf_op jit(solution)/shard_map/all_to_all | solution.py:187
  258.9 6.1 copy-start.29
  258.9 101.1 %copy-start.30 = (bf16[384,128]{1,0:T(8,128)(2,1)S(1)}, bf16[384,128]{1,0:T(8,128)(2,1)}, u32[]{:S(2)}) copy-start(bf16[384,128]{1,0:T(8,128)(2,1)} %param.28) | copy-start | bytes 294916
  258.9 141.3 %copy-start.31 = (bf16[128,512]{1,0:T(8,128)(2,1)S(1)}, bf16[128,512]{1,0:T(8,128)(2,1)}, u32[]{:S(2)}) copy-start(bf16[128,512]{1,0:T(8,128)(2,1)} %param.23) | copy-start | bytes 393220
  258.9 141.3 %copy-start.32 = (bf16[128,512]{1,0:T(8,128)(2,1)S(1)}, bf16[128,512]{1,0:T(8,128)(2,1)}, u32[]{:S(2)}) copy-start(bf16[128,512]{1,0:T(8,128)(2,1)} %param.22) | copy-start | bytes 393220
  258.9 688.2 %reduce-scatter.2.cloned.1.call-start = ((), (), s32[]{:S(2)}) async-start(), calls=%async_computation.4 | async-start | bytes 73728 | tf_op jit(solution)/shard_map/reduce_scatter | solution.py:238
  262.3 137.8 %copy-start.23 = (f32[32,1536]{1,0:T(8,128)}, f32[32,1536]{1,0:T(8,128)S(1)}, u32[]{:S(2)}) copy-start(f32[32,1536]{1,0:T(8,128)S(1)} %fusion.52) | copy-start | bytes 589828
  263.4 96.7 %copy-start.21 = (bf16[32,1536]{1,0:T(8,128)(2,1)}, bf16[32,1536]{1,0:T(8,128)(2,1)S(1)}, u32[]{:S(2)}) copy-start(bf16[32,1536]{1,0:T(8,128)(2,1)S(1)} %get-tuple-element.350) | copy-start | bytes 294916
  265.0 135.1 %copy-start.24 = (bf16[32,384]{1,0:T(8,128)(2,1)}, bf16[32,384]{1,0:T(8,128)(2,1)S(1)}, u32[]{:S(2)}) copy-start(bf16[32,384]{1,0:T(8,128)(2,1)S(1)} %fusion.26) | copy-start | bytes 73732
  400.9 6.5 copy-start.13
  425.9 27.5 %copy-start.6 = (bf16[1,64,128,128]{3,2,1,0:T(8,128)(2,1)}, bf16[1,64,128,128]{3,2,1,0:T(8,128)(2,1)S(1)}, u32[]{:S(2)}) copy-start(bf16[1,64,128,128]{3,2,1,0:T(8,128)(2,1)S(1)} %get-tuple-element.483) | copy-start | bytes 6291460 | tf_op jit(solution)/shard_map/while
  431.3 14.7 %copy-start.1 = (f32[8192,128]{1,0:T(8,128)}, f32[8192,128]{1,0:T(8,128)S(1)}, u32[]{:S(2)}) copy-start(f32[8192,128]{1,0:T(8,128)S(1)} %get-tuple-element.485) | copy-start | bytes 12582916 | tf_op jit(solution)/shard_map/while
  453.4 3.2 copy-start.8
  456.7 22.8 %copy-start.2 = (f32[8192,128]{1,0:T(8,128)S(1)}, f32[8192,128]{1,0:T(8,128)}, u32[]{:S(2)}) copy-start(f32[8192,128]{1,0:T(8,128)} %copy-done.1) | copy-start | bytes 12582916 | tf_op jit(solution)/shard_map/while
  456.7 22.8 %copy-start.10 = (bf16[128,1024]{1,0:T(8,128)(2,1)S(1)}, bf16[128,1024]{1,0:T(8,128)(2,1)}, u32[]{:S(2)}) copy-start(bf16[128,1024]{1,0:T(8,128)(2,1)} %get-tuple-element.557) | copy-start | bytes 786436 | tf_op jit(solution)/shard_map/while
  479.4 13.3 %copy-start.5 = (f32[8192,128]{1,0:T(8,128)S(1)}, f32[8192,128]{1,0:T(8,128)}, u32[]{:S(2)}) copy-start(f32[8192,128]{1,0:T(8,128)} %fusion.124) | copy-start | bytes 12582916 | tf_op jit(solution)/shard_map/while
  497.7 2.8 copy-start.4
  497.7 3.1 copy-start.7
  512.1 7.8 copy-start.3
  512.1 7.8 copy-start.26
  532.4 6.9 copy-start.27
  535.1 4.9 copy-start.15
  542.5 27.5 %copy-start.6 = (bf16[1,64,128,128]{3,2,1,0:T(8,128)(2,1)}, bf16[1,64,128,128]{3,2,1,0:T(8,128)(2,1)S(1)}, u32[]{:S(2)}) copy-start(bf16[1,64,128,128]{3,2,1,0:T(8,128)(2,1)S(1)} %get-tuple-element.483) | copy-start | bytes 6291460 | tf_op jit(solution)/shard_map/while
  547.8 14.7 %copy-start.1 = (f32[8192,128]{1,0:T(8,128)}, f32[8192,128]{1,0:T(8,128)S(1)}, u32[]{:S(2)}) copy-start(f32[8192,128]{1,0:T(8,128)S(1)} %get-tuple-element.485) | copy-start | bytes 12582916 | tf_op jit(solution)/shard_map/while
  570.0 3.2 copy-start.8
  573.2 22.8 %copy-start.2 = (f32[8192,128]{1,0:T(8,128)S(1)}, f32[8192,128]{1,0:T(8,128)}, u32[]{:S(2)}) copy-start(f32[8192,128]{1,0:T(8,128)} %copy-done.1) | copy-start | bytes 12582916 | tf_op jit(solution)/shard_map/while
  573.2 22.8 %copy-start.10 = (bf16[128,1024]{1,0:T(8,128)(2,1)S(1)}, bf16[128,1024]{1,0:T(8,128)(2,1)}, u32[]{:S(2)}) copy-start(bf16[128,1024]{1,0:T(8,128)(2,1)} %get-tuple-element.557) | copy-start | bytes 786436 | tf_op jit(solution)/shard_map/while
  596.0 13.3 %copy-start.5 = (f32[8192,128]{1,0:T(8,128)S(1)}, f32[8192,128]{1,0:T(8,128)}, u32[]{:S(2)}) copy-start(f32[8192,128]{1,0:T(8,128)} %fusion.124) | copy-start | bytes 12582916 | tf_op jit(solution)/shard_map/while
  614.3 3.1 copy-start.7
  628.6 7.8 copy-start.3
  628.6 7.8 copy-start.26
  649.0 6.9 copy-start.27
  651.7 4.9 copy-start.15
  659.0 27.5 %copy-start.6 = (bf16[1,64,128,128]{3,2,1,0:T(8,128)(2,1)}, bf16[1,64,128,128]{3,2,1,0:T(8,128)(2,1)S(1)}, u32[]{:S(2)}) copy-start(bf16[1,64,128,128]{3,2,1,0:T(8,128)(2,1)S(1)} %get-tuple-element.483) | copy-start | bytes 6291460 | tf_op jit(solution)/shard_map/while
  664.4 14.7 %copy-start.1 = (f32[8192,128]{1,0:T(8,128)}, f32[8192,128]{1,0:T(8,128)S(1)}, u32[]{:S(2)}) copy-start(f32[8192,128]{1,0:T(8,128)S(1)} %get-tuple-element.485) | copy-start | bytes 12582916 | tf_op jit(solution)/shard_map/while
  686.5 3.2 copy-start.8
  689.8 22.8 %copy-start.2 = (f32[8192,128]{1,0:T(8,128)S(1)}, f32[8192,128]{1,0:T(8,128)}, u32[]{:S(2)}) copy-start(f32[8192,128]{1,0:T(8,128)} %copy-done.1) | copy-start | bytes 12582916 | tf_op jit(solution)/shard_map/while
  689.8 22.8 %copy-start.10 = (bf16[128,1024]{1,0:T(8,128)(2,1)S(1)}, bf16[128,1024]{1,0:T(8,128)(2,1)}, u32[]{:S(2)}) copy-start(bf16[128,1024]{1,0:T(8,128)(2,1)} %get-tuple-element.557) | copy-start | bytes 786436 | tf_op jit(solution)/shard_map/while
  712.5 13.3 %copy-start.5 = (f32[8192,128]{1,0:T(8,128)S(1)}, f32[8192,128]{1,0:T(8,128)}, u32[]{:S(2)}) copy-start(f32[8192,128]{1,0:T(8,128)} %fusion.124) | copy-start | bytes 12582916 | tf_op jit(solution)/shard_map/while
  730.8 3.1 copy-start.7
  745.2 7.8 copy-start.3
  745.2 7.8 copy-start.26
  765.5 6.9 copy-start.27
  768.2 4.9 copy-start.15
  775.6 27.5 %copy-start.6 = (bf16[1,64,128,128]{3,2,1,0:T(8,128)(2,1)}, bf16[1,64,128,128]{3,2,1,0:T(8,128)(2,1)S(1)}, u32[]{:S(2)}) copy-start(bf16[1,64,128,128]{3,2,1,0:T(8,128)(2,1)S(1)} %get-tuple-element.483) | copy-start | bytes 6291460 | tf_op jit(solution)/shard_map/while
  780.9 14.7 %copy-start.1 = (f32[8192,128]{1,0:T(8,128)}, f32[8192,128]{1,0:T(8,128)S(1)}, u32[]{:S(2)}) copy-start(f32[8192,128]{1,0:T(8,128)S(1)} %get-tuple-element.485) | copy-start | bytes 12582916 | tf_op jit(solution)/shard_map/while
  803.1 3.2 copy-start.8
  806.3 22.8 %copy-start.2 = (f32[8192,128]{1,0:T(8,128)S(1)}, f32[8192,128]{1,0:T(8,128)}, u32[]{:S(2)}) copy-start(f32[8192,128]{1,0:T(8,128)} %copy-done.1) | copy-start | bytes 12582916 | tf_op jit(solution)/shard_map/while
  806.3 22.8 %copy-start.10 = (bf16[128,1024]{1,0:T(8,128)(2,1)S(1)}, bf16[128,1024]{1,0:T(8,128)(2,1)}, u32[]{:S(2)}) copy-start(bf16[128,1024]{1,0:T(8,128)(2,1)} %get-tuple-element.557) | copy-start | bytes 786436 | tf_op jit(solution)/shard_map/while
  829.1 13.3 %copy-start.5 = (f32[8192,128]{1,0:T(8,128)S(1)}, f32[8192,128]{1,0:T(8,128)}, u32[]{:S(2)}) copy-start(f32[8192,128]{1,0:T(8,128)} %fusion.124) | copy-start | bytes 12582916 | tf_op jit(solution)/shard_map/while
  847.4 3.1 copy-start.7
  861.7 7.8 copy-start.3
  861.7 7.8 copy-start.26
  882.1 6.9 copy-start.27
  884.7 4.9 copy-start.15
  889.8 62.7 %copy-start.17 = (bf16[32,384]{1,0:T(8,128)(2,1)S(1)}, bf16[32,384]{1,0:T(8,128)(2,1)}, u32[]{:S(2)}) copy-start(bf16[32,384]{1,0:T(8,128)(2,1)} %param.20) | copy-start | bytes 73732
  889.8 62.7 %copy-start.35 = (f32[32]{0:T(128)S(1)}, f32[32]{0:T(128)}, u32[]{:S(2)}) copy-start(f32[32]{0:T(128)} %copy-done.34) | copy-start | bytes 388
  918.9 218.1 %all-reduce.3.cloned.1.call-start = ((), (), s32[]{:S(2)}) async-start(), calls=%async_computation.5 | async-start | bytes 16646144 | tf_op jit(solution)/shard_map/psum | solution.py:256
  953.7 3.5 copy-start.25
  953.7 3.4 copy-start.33
  958.0 41.4 %copy-start.12 = (bf16[384,1536]{1,0:T(8,128)(2,1)S(1)}, bf16[384,1536]{1,0:T(8,128)(2,1)}, u32[]{:S(2)}) copy-start(bf16[384,1536]{1,0:T(8,128)(2,1)} %param.29) | copy-start | bytes 3538948
  (29 other events, 57.1 us)
Sparse Core Ops, SparseCore 0:
  919.0 28.1 reduce-scatter.1
  958.1 178.7 all-reduce.2
where the time goes:
time: 1170 us; the launch traced here: 1150 us
  blocking collectives  402 us (34%)
  matrix products  371 us (32%)
  waiting for transfers between devices  162 us (14%)
  local copies, waits for them, and re-layouts  102 us (9%)
  other arithmetic  81.1 us (7%)
  loops' own time  17.3 us (1%)
  between operations  14.7 us (1%)
    dot_general x17, matrix products, product_right(): lax.dot_general(matrix_a, matrix_b, (((1,), (1,)), ((), ())), preferred_e...  162 us
    psum x1, waiting for transfers between devices, local(): lax.psum((up_gate_sum, down_sum, head_sum, rel_sum, prow_sum, pcol_sum),...  136 us
    dot_general x17, matrix products, product_left(): lax.dot_general(matrix_a, matrix_b, (((0,), (0,)), ((), ())), preferred_e...  131 us
    all_to_all x1, blocking collectives, local(): lax.all_to_all(distance_part, 'col', split_axis=0, concat_axis=1, tiled=T...  100 us
    all_to_all x1, blocking collectives, local(): lax.all_to_all(strips, ('row', 'col'), split_axis=1, concat_axis=0, tiled...  98.3 us
    all_gather x1, blocking collectives, local(): row_proj = lax.all_gather(row_piece, 'col', axis=0, tiled=True)  94.8 us
    dot_general x13, matrix products, product(): return jnp.dot(matrix_a, matrix_b, preferred_element_type=jnp.float32)  61.4 us
    all_gather x1, blocking collectives, local(): col_whole = lax.all_gather(col_piece, ('row', 'col'), axis=0, tiled=True)  40 us
  transfers between devices with their start and end apart: 3, of which 2 were waited for; matrix products, arithmetic and copies ran while one was open for 1% of the time, Pallas kernels for 0%

commit v1 on v0

--- a/solution.py
+++ b/solution.py
@@ -183,7 +183,10 @@
     masked = logit_cotangent * pair_mask[:, :, None].astype(jnp.bfloat16)
     distance_part = masked[:, :, bin_count:].reshape(tile_rows, tile_cols * bin_count)
     strips = lax.all_to_all(distance_part, "col", split_axis=0, concat_axis=1, tiled=True)
-    columns = lax.all_to_all(strips, ("row", "col"), split_axis=1, concat_axis=0, tiled=True)
+    n_dev = lax.axis_size(("row", "col"))
+    shards = jnp.stack(jnp.split(strips, n_dev, axis=1), axis=0)
+    shards = lax.all_to_all(shards, ("row", "col"), split_axis=0, concat_axis=0)
+    columns = jnp.concatenate(shards, axis=0)
     returned = lax.all_to_all(columns, "col", split_axis=0, concat_axis=1, tiled=True)
     mirrored = returned.reshape(tile_cols, tile_rows, bin_count).transpose(1, 0, 2)
     up_gate = jnp.concatenate([pair_up, pair_gate], axis=1)

time: 1170 us -> 1150 us (0.983)
  local copies, waits for them, and re-layouts: 102 us -> 85.6 us
    all_to_all x2 -> x0, local copies, waits for them, and re-layouts: 12.4 us -> none  [local(): lax.all_to_all(strips, ('row', 'col'), split_axis=1, concat_axis=0, tiled...]
where the time goes in v1:
time: 1150 us; the launch traced here: 1140 us
  blocking collectives  402 us (35%)
  matrix products  371 us (32%)
  waiting for transfers between devices  162 us (14%)
  local copies, waits for them, and re-layouts  85.6 us (7%)
  other arithmetic  81.1 us (7%)
  loops' own time  17.3 us (2%)
  between operations  15 us (1%)
    dot_general x17, matrix products, product_right(): lax.dot_general(matrix_a, matrix_b, (((1,), (1,)), ((), ())), preferred_e...  162 us
    psum x1, waiting for transfers between devices, local(): lax.psum((up_gate_sum, down_sum, head_sum, rel_sum, prow_sum, pcol_sum),...  136 us
    dot_general x17, matrix products, product_left(): lax.dot_general(matrix_a, matrix_b, (((0,), (0,)), ((), ())), preferred_e...  131 us
    all_to_all x1, blocking collectives, local(): lax.all_to_all(distance_part, 'col', split_axis=0, concat_axis=1, tiled=T...  100 us
    all_to_all x1, blocking collectives, local(): shards = lax.all_to_all(shards, ('row', 'col'), split_axis=0, concat_axis=0)  98.3 us
    all_gather x1, blocking collectives, local(): row_proj = lax.all_gather(row_piece, 'col', axis=0, tiled=True)  94.7 us
    dot_general x13, matrix products, product(): return jnp.dot(matrix_a, matrix_b, preferred_element_type=jnp.float32)  61.4 us
    psum x1, blocking collectives, local(): lax.psum((up_gate_sum, down_sum, head_sum, rel_sum, prow_sum, pcol_sum),...  40 us
  transfers between devices with their start and end apart: 3, of which 2 were waited for; matrix products, arithmetic and copies ran while one was open for 1% of the time, Pallas kernels for 0%

profile of v1, /device:TPU:0, one launch (start us, length us, event | category | flops | bytes accessed | tf_op | source)
XLA Modules:
  0.0 1139.0 jit_solution(9900168258754778855)
XLA Ops:
  8.2 8.6 broadcast_multiply_fusion.3
  16.8 9.9 slice.44
  26.8 12.1 %all_to_all.29 = bf16[8,32,8192]{2,1,0:T(8,128)(2,1)} reshape(bf16[256,128,64]{2,1,0:T(8,128)(2,1)} %slice.44) | data formatting | bytes 8388608 | tf_op jit(solution)/shard_map/all_to_all | solution.py:185
  38.8 100.3 %all_to_all.40 = bf16[8,32,8192]{2,1,0:T(8,128)(2,1)S(1)} all-to-all(bf16[8,32,8192]{2,1,0:T(8,128)(2,1)} %all_to_all.29), channel_id=1, replica_groups=mesh['row'=4,'col'=8] {'col'}, dimensions={0} | all-to-all | bytes 8388608 | tf_op jit(solution)/shard_map/all_to_all | solution.py:185
  140.2 98.3 %all_to_all.41 = bf16[32,32,2048]{2,1,0:T(8,128)(2,1)} all-to-all(bf16[32,32,2048]{2,1,0:T(8,128)(2,1)S(1)} %fusion.31), channel_id=1, replica_groups=mesh['row'=4,'col'=8] {'row','col'}, dimensions={0} | all-to-all | bytes 8388608 | tf_op jit(solution)/shard_map/all_to_all | solution.py:188
  238.5 6.5 copy.37
  245.0 4.7 all-to-all-start.2
  256.0 94.7 %all_gather.9 = bf16[256,128]{1,0:T(8,128)(2,1)} all-gather(bf16[32,128]{1,0:T(8,128)(2,1)S(1)} %convolution_convert_fusion.1), channel_id=1, replica_groups=mesh['row'=4,'col'=8] {'col'}, dimensions={0}, use_global_device_ids=true | all-gather | bytes 73728 | tf_op jit(solution)/shard_map/all_gather | solution.py:180
  350.9 40.0 %all_gather.10 = bf16[1024,128]{1,0:T(8,128)(2,1)S(1)} all-gather(bf16[32,128]{1,0:T(8,128)(2,1)S(1)} %convolution_convert_fusion), channel_id=1, replica_groups=mesh['row'=4,'col'=8] {'row','col'}, dimensions={0}, use_global_device_ids=true | all-gather | bytes 270336 | tf_op jit(solution)/shard_map/all_gather | solution.py:181
  391.7 482.4 %while.23 = (s32[]{:T(128)}, f32[128,128]{1,0:T(8,128)}, f32[128,1024]{1,0:T(8,128)}, f32[512,128]{1,0:T(8,128)}, f32[128,128]{1,0:T(8,128)}, /*index=5*/f32[65,...) while((s32[]{:T(128)}, f32[128,128]{1,0:T(8,128)}, ...), condition=%wide.region_8.9_spmd.clone, body=%wide.region_1.8_spmd.clone.sunk | while | flops 11331420160 | bytes 375022848 | solution.py:236
  407.9 2.5 constant_dynamic-slice_fusion.7
  418.3 12.2 %fusion.159 = f32[8192,1024]{0,1:T(8,128)} fusion(bf16[128,1024]{1,0:T(8,128)(2,1)S(1)} %copy-done.9, f32[8192,128]{1,0:T(8,128)S(1)} %get-tuple-element.454, f32[8192]{0:T(1024)S(1)} %add_rsqrt_fusion.3, f32[8192]{0:T(1024)S(1)} %broadcast_multiply_fusion.13), kind=kOutput, calls=%fused_computation.53.clone.1 | convolution fusion | flops 2150629376 | bytes 38076416 | tf_op jit(solution)/shard_map/while/body/eval_jaxpr/dot_general | solution.py:15
  432.8 2.7 copy.45
  437.9 3.2 fusion.156
  441.1 22.8 %multiply_convert_fusion.7 = (bf16[8192,512]{0,1:T(8,128)(2,1)}, bf16[8192,512]{0,1:T(8,128)(2,1)}, bf16[8192,512]{0,1:T(8,128)(2,1)}) fusion(f32[8192,1024]{0,1:T(8,128)} %fusion.159, bf16[512,128]{1,0:T(8,128)(2,1)S(1)} %get-tuple-element.525, f32[8192,128]{1,0:T(8,128)} %fusion.156), kind=kOutput, calls=%fused_computation.3.clone.1 | convolution fusion | flops 1137704960 | bytes 63045632 | tf_op jit(solution)/shard_map/while/body/eval_jaxpr/dot_general | solution.py:25
  463.9 13.2 %fusion.160 = (f32[8192]{0:T(1024)S(1)}, f32[8192]{0:T(1024)S(1)}, f32[8192,128]{1,0:T(8,128)S(1)}) fusion(f32[8192]{0:T(1024)S(1)} %add_rsqrt_fusion.3, f32[8192,128]{1,0:T(8,128)S(1)} %copy-done.2, f32[8192]{0:T(1024)S(1)} %broadcast_multiply_fusion.13, bf16[128,1024]{1,0:T(8,128)(2,1)S(1)} %copy-done.10, ...), kind=kOutput, calls=%fused_computation.172.clone.1 | convolution fusion | flops 2186264576 | bytes 25559040 | tf_op jit(solution)/shard_map/while/body/eval_jaxpr/dot_general | solution.py:25
  477.2 5.0 bitcast_reduce_fusion.2
  485.3 11.2 fusion.162
  496.6 7.8 convolution_add_fusion.7
  504.3 12.5 %fusion.161 = f32[128,1024]{1,0:T(8,128)S(1)} fusion(bf16[8192,512]{0,1:T(8,128)(2,1)} %get-tuple-element.456, bf16[8192,512]{0,1:T(8,128)(2,1)} %get-tuple-element.457, f32[128,1024]{1,0:T(8,128)S(1)} %copy-done.26, pred[]{:T(512)S(6)} %compare.3, f32[8192,128]{1,0:T(8,128)S(1)} %copy-done.3, f32[8192]{0:T(1024)S(1)} %add_rsqrt_fusion.3, ...), kind=kOutput, calls=%fused_computation.23.clone.1 | convolution fusion | flops 2184445952 | bytes 22085632 | tf_op jit(solution)/shard_map/while/body/eval_jaxpr/dot_general | solution.py:19
  516.9 2.6 reduce_sum.96
  519.6 4.2 fusion.163
  524.4 2.5 constant_dynamic-slice_fusion.7
  534.8 12.2 %fusion.159 = f32[8192,1024]{0,1:T(8,128)} fusion(bf16[128,1024]{1,0:T(8,128)(2,1)S(1)} %copy-done.9, f32[8192,128]{1,0:T(8,128)S(1)} %get-tuple-element.454, f32[8192]{0:T(1024)S(1)} %add_rsqrt_fusion.3, f32[8192]{0:T(1024)S(1)} %broadcast_multiply_fusion.13), kind=kOutput, calls=%fused_computation.53.clone.1 | convolution fusion | flops 2150629376 | bytes 38076416 | tf_op jit(solution)/shard_map/while/body/eval_jaxpr/dot_general | solution.py:15
  549.3 2.7 copy.45
  554.5 3.2 fusion.156
  557.7 22.8 %multiply_convert_fusion.7 = (bf16[8192,512]{0,1:T(8,128)(2,1)}, bf16[8192,512]{0,1:T(8,128)(2,1)}, bf16[8192,512]{0,1:T(8,128)(2,1)}) fusion(f32[8192,1024]{0,1:T(8,128)} %fusion.159, bf16[512,128]{1,0:T(8,128)(2,1)S(1)} %get-tuple-element.525, f32[8192,128]{1,0:T(8,128)} %fusion.156), kind=kOutput, calls=%fused_computation.3.clone.1 | convolution fusion | flops 1137704960 | bytes 63045632 | tf_op jit(solution)/shard_map/while/body/eval_jaxpr/dot_general | solution.py:25
  580.5 13.2 %fusion.160 = (f32[8192]{0:T(1024)S(1)}, f32[8192]{0:T(1024)S(1)}, f32[8192,128]{1,0:T(8,128)S(1)}) fusion(f32[8192]{0:T(1024)S(1)} %add_rsqrt_fusion.3, f32[8192,128]{1,0:T(8,128)S(1)} %copy-done.2, f32[8192]{0:T(1024)S(1)} %broadcast_multiply_fusion.13, bf16[128,1024]{1,0:T(8,128)(2,1)S(1)} %copy-done.10, ...), kind=kOutput, calls=%fused_computation.172.clone.1 | convolution fusion | flops 2186264576 | bytes 25559040 | tf_op jit(solution)/shard_map/while/body/eval_jaxpr/dot_general | solution.py:25
  593.7 5.0 bitcast_reduce_fusion.2
  601.9 11.2 fusion.162
  613.1 7.8 convolution_add_fusion.7
  620.9 12.5 %fusion.161 = f32[128,1024]{1,0:T(8,128)S(1)} fusion(bf16[8192,512]{0,1:T(8,128)(2,1)} %get-tuple-element.456, bf16[8192,512]{0,1:T(8,128)(2,1)} %get-tuple-element.457, f32[128,1024]{1,0:T(8,128)S(1)} %copy-done.26, pred[]{:T(512)S(6)} %compare.3, f32[8192,128]{1,0:T(8,128)S(1)} %copy-done.3, f32[8192]{0:T(1024)S(1)} %add_rsqrt_fusion.3, ...), kind=kOutput, calls=%fused_computation.23.clone.1 | convolution fusion | flops 2184445952 | bytes 22085632 | tf_op jit(solution)/shard_map/while/body/eval_jaxpr/dot_general | solution.py:19
  633.5 2.6 reduce_sum.96
  636.1 4.2 fusion.163
  641.0 2.5 constant_dynamic-slice_fusion.7
  651.4 12.2 %fusion.159 = f32[8192,1024]{0,1:T(8,128)} fusion(bf16[128,1024]{1,0:T(8,128)(2,1)S(1)} %copy-done.9, f32[8192,128]{1,0:T(8,128)S(1)} %get-tuple-element.454, f32[8192]{0:T(1024)S(1)} %add_rsqrt_fusion.3, f32[8192]{0:T(1024)S(1)} %broadcast_multiply_fusion.13), kind=kOutput, calls=%fused_computation.53.clone.1 | convolution fusion | flops 2150629376 | bytes 38076416 | tf_op jit(solution)/shard_map/while/body/eval_jaxpr/dot_general | solution.py:15
  665.9 2.7 copy.45
  671.0 3.2 fusion.156
  674.2 22.8 %multiply_convert_fusion.7 = (bf16[8192,512]{0,1:T(8,128)(2,1)}, bf16[8192,512]{0,1:T(8,128)(2,1)}, bf16[8192,512]{0,1:T(8,128)(2,1)}) fusion(f32[8192,1024]{0,1:T(8,128)} %fusion.159, bf16[512,128]{1,0:T(8,128)(2,1)S(1)} %get-tuple-element.525, f32[8192,128]{1,0:T(8,128)} %fusion.156), kind=kOutput, calls=%fused_computation.3.clone.1 | convolution fusion | flops 1137704960 | bytes 63045632 | tf_op jit(solution)/shard_map/while/body/eval_jaxpr/dot_general | solution.py:25
  697.0 13.2 %fusion.160 = (f32[8192]{0:T(1024)S(1)}, f32[8192]{0:T(1024)S(1)}, f32[8192,128]{1,0:T(8,128)S(1)}) fusion(f32[8192]{0:T(1024)S(1)} %add_rsqrt_fusion.3, f32[8192,128]{1,0:T(8,128)S(1)} %copy-done.2, f32[8192]{0:T(1024)S(1)} %broadcast_multiply_fusion.13, bf16[128,1024]{1,0:T(8,128)(2,1)S(1)} %copy-done.10, ...), kind=kOutput, calls=%fused_computation.172.clone.1 | convolution fusion | flops 2186264576 | bytes 25559040 | tf_op jit(solution)/shard_map/while/body/eval_jaxpr/dot_general | solution.py:25
  710.3 5.0 bitcast_reduce_fusion.2
  718.4 11.2 fusion.162
  729.6 7.8 convolution_add_fusion.7
  737.4 12.5 %fusion.161 = f32[128,1024]{1,0:T(8,128)S(1)} fusion(bf16[8192,512]{0,1:T(8,128)(2,1)} %get-tuple-element.456, bf16[8192,512]{0,1:T(8,128)(2,1)} %get-tuple-element.457, f32[128,1024]{1,0:T(8,128)S(1)} %copy-done.26, pred[]{:T(512)S(6)} %compare.3, f32[8192,128]{1,0:T(8,128)S(1)} %copy-done.3, f32[8192]{0:T(1024)S(1)} %add_rsqrt_fusion.3, ...), kind=kOutput, calls=%fused_computation.23.clone.1 | convolution fusion | flops 2184445952 | bytes 22085632 | tf_op jit(solution)/shard_map/while/body/eval_jaxpr/dot_general | solution.py:19
  750.0 2.6 reduce_sum.96
  752.7 4.2 fusion.163
  757.5 2.5 constant_dynamic-slice_fusion.7
  767.9 12.2 %fusion.159 = f32[8192,1024]{0,1:T(8,128)} fusion(bf16[128,1024]{1,0:T(8,128)(2,1)S(1)} %copy-done.9, f32[8192,128]{1,0:T(8,128)S(1)} %get-tuple-element.454, f32[8192]{0:T(1024)S(1)} %add_rsqrt_fusion.3, f32[8192]{0:T(1024)S(1)} %broadcast_multiply_fusion.13), kind=kOutput, calls=%fused_computation.53.clone.1 | convolution fusion | flops 2150629376 | bytes 38076416 | tf_op jit(solution)/shard_map/while/body/eval_jaxpr/dot_general | solution.py:15
  782.4 2.7 copy.45
  787.6 3.2 fusion.156
  790.8 22.8 %multiply_convert_fusion.7 = (bf16[8192,512]{0,1:T(8,128)(2,1)}, bf16[8192,512]{0,1:T(8,128)(2,1)}, bf16[8192,512]{0,1:T(8,128)(2,1)}) fusion(f32[8192,1024]{0,1:T(8,128)} %fusion.159, bf16[512,128]{1,0:T(8,128)(2,1)S(1)} %get-tuple-element.525, f32[8192,128]{1,0:T(8,128)} %fusion.156), kind=kOutput, calls=%fused_computation.3.clone.1 | convolution fusion | flops 1137704960 | bytes 63045632 | tf_op jit(solution)/shard_map/while/body/eval_jaxpr/dot_general | solution.py:25
  813.6 13.2 %fusion.160 = (f32[8192]{0:T(1024)S(1)}, f32[8192]{0:T(1024)S(1)}, f32[8192,128]{1,0:T(8,128)S(1)}) fusion(f32[8192]{0:T(1024)S(1)} %add_rsqrt_fusion.3, f32[8192,128]{1,0:T(8,128)S(1)} %copy-done.2, f32[8192]{0:T(1024)S(1)} %broadcast_multiply_fusion.13, bf16[128,1024]{1,0:T(8,128)(2,1)S(1)} %copy-done.10, ...), kind=kOutput, calls=%fused_computation.172.clone.1 | convolution fusion | flops 2186264576 | bytes 25559040 | tf_op jit(solution)/shard_map/while/body/eval_jaxpr/dot_general | solution.py:25
  826.8 5.0 bitcast_reduce_fusion.2
  835.0 11.2 fusion.162
  846.2 7.8 convolution_add_fusion.7
  854.0 12.5 %fusion.161 = f32[128,1024]{1,0:T(8,128)S(1)} fusion(bf16[8192,512]{0,1:T(8,128)(2,1)} %get-tuple-element.456, bf16[8192,512]{0,1:T(8,128)(2,1)} %get-tuple-element.457, f32[128,1024]{1,0:T(8,128)S(1)} %copy-done.26, pred[]{:T(512)S(6)} %compare.3, f32[8192,128]{1,0:T(8,128)S(1)} %copy-done.3, f32[8192]{0:T(1024)S(1)} %add_rsqrt_fusion.3, ...), kind=kOutput, calls=%fused_computation.23.clone.1 | convolution fusion | flops 2184445952 | bytes 22085632 | tf_op jit(solution)/shard_map/while/body/eval_jaxpr/dot_general | solution.py:19
  866.6 2.6 reduce_sum.96
  869.2 4.2 fusion.163
  874.9 14.0 %psum.56 = bf16[128,128]{1,0:T(8,128)(2,1)S(1)} all-reduce(bf16[128,128]{1,0:T(8,128)(2,1)S(1)} %convert_element_type.121), channel_id=1, replica_groups=mesh['row'=4,'col'=8] {'row'}, use_global_device_ids=true, to_apply=%region_10.11 | all-reduce | flops 16384 | bytes 65536 | tf_op jit(solution)/shard_map/psum | solution.py:244
  888.9 14.2 %all_gather.11 = bf16[1024,128]{1,0:T(8,128)(2,1)S(1)} all-gather(bf16[128,128]{1,0:T(8,128)(2,1)S(1)} %psum.56), channel_id=1, replica_groups=mesh['row'=4,'col'=8] {'col'}, dimensions={0}, use_global_device_ids=true | all-gather | bytes 294912 | tf_op jit(solution)/shard_map/all_gather | solution.py:245
  904.8 26.6 %reduce-scatter.2.cloned.1.call-done = bf16[32,128]{1,0:T(8,128)(2,1)} async-done(((bf16[256,128]{1,0:T(8,128)(2,1)}), bf16[32,128]{1,0:T(8,128)(2,1)}) %reduce-scatter.2.cloned.1.call-update) | async-done | bytes 8208 | tf_op jit(solution)/shard_map/reduce_scatter | solution.py:241
  937.9 3.4 pad_maximum_fusion.8
  943.0 40.0 %psum.60 = f32[65,128]{1,0:T(8,128)S(1)} all-reduce(f32[65,128]{1,0:T(8,128)S(1)} %copy-done.20), channel_id=1, replica_groups=mesh['row'=4,'col'=8] {'row','col'}, use_global_device_ids=true, to_apply=%region_15.16 | all-reduce | flops 8320 | bytes 66560 | tf_op jit(solution)/shard_map/psum | solution.py:259
  985.5 135.8 %all-reduce.3.cloned.1.call-done = (f32[128,1024]{1,0:T(8,128)}, f32[512,128]{1,0:T(8,128)}, f32[128,128]{1,0:T(8,128)}, f32[384,128]{1,0:T(8,128)}, f32[384,128]{1,0:T(8,128)}, /*index=5*/f32[3,384,1536]{2,1,0:T(8,128)}) async-done(((f32[128,1024]{1,0:T(8,128)}, f32[512,128]{1,0:T(8,128)}, f32[128,128]{1,0:T(8,128)}, f32[384,128]{1,0:T(8,128)}, f32[384,128]{1,0:T(8,128)}, ...) | async-done | bytes 8323088 | tf_op jit(solution)/shard_map/psum | solution.py:259
  (328 shorter events, 97.3 us)
Async XLA Ops:
  7.2 246.0 %copy-start = (bf16[384,1536]{1,0:T(8,128)(2,1)S(1)}, bf16[384,1536]{1,0:T(8,128)(2,1)}, u32[]{:S(2)}) copy-start(bf16[384,1536]{1,0:T(8,128)(2,1)} %param.30) | copy-start | bytes 3538948
  245.0 7.8 copy-start.16
  245.0 7.9 copy-start.11
  245.0 146.7 %all-to-all-start.2 = ((bf16[8,128,2048]{1,2,0:T(8,128)(2,1)}), bf16[8,128,2048]{1,2,0:T(8,128)(2,1)}, u32[]{:S(2)}, u32[]{:S(2)}) async-start(bf16[8,128,2048]{1,2,0:T(8,128)(2,1)} %copy.37), calls=%async_computation.2 | async-start | bytes 8388608 | tf_op jit(solution)/shard_map/all_to_all | solution.py:190
  249.7 6.2 copy-start.29
  249.7 101.1 %copy-start.30 = (bf16[384,128]{1,0:T(8,128)(2,1)S(1)}, bf16[384,128]{1,0:T(8,128)(2,1)}, u32[]{:S(2)}) copy-start(bf16[384,128]{1,0:T(8,128)(2,1)} %param.28) | copy-start | bytes 294916
  249.7 141.2 %copy-start.31 = (bf16[128,512]{1,0:T(8,128)(2,1)S(1)}, bf16[128,512]{1,0:T(8,128)(2,1)}, u32[]{:S(2)}) copy-start(bf16[128,512]{1,0:T(8,128)(2,1)} %param.23) | copy-start | bytes 393220
  249.7 141.2 %copy-start.32 = (bf16[128,512]{1,0:T(8,128)(2,1)S(1)}, bf16[128,512]{1,0:T(8,128)(2,1)}, u32[]{:S(2)}) copy-start(bf16[128,512]{1,0:T(8,128)(2,1)} %param.22) | copy-start | bytes 393220
  249.7 141.9 %copy-start.13 = (bf16[512,128]{1,0:T(8,128)(2,1)S(1)}, bf16[512,128]{1,0:T(8,128)(2,1)}, u32[]{:S(2)}) copy-start(bf16[512,128]{1,0:T(8,128)(2,1)} %param.24) | copy-start | bytes 393220
  249.7 681.7 %reduce-scatter.2.cloned.1.call-start = ((), (), s32[]{:S(2)}) async-start(), calls=%async_computation.4 | async-start | bytes 73728 | tf_op jit(solution)/shard_map/reduce_scatter | solution.py:241
  253.2 138.4 %copy-start.23 = (f32[32,1536]{1,0:T(8,128)}, f32[32,1536]{1,0:T(8,128)S(1)}, u32[]{:S(2)}) copy-start(f32[32,1536]{1,0:T(8,128)S(1)} %fusion.84) | copy-start | bytes 589828
  254.3 137.4 %copy-start.21 = (bf16[32,1536]{1,0:T(8,128)(2,1)}, bf16[32,1536]{1,0:T(8,128)(2,1)S(1)}, u32[]{:S(2)}) copy-start(bf16[32,1536]{1,0:T(8,128)(2,1)S(1)} %get-tuple-element.319) | copy-start | bytes 294916
  255.9 135.8 %copy-start.24 = (bf16[32,384]{1,0:T(8,128)(2,1)}, bf16[32,384]{1,0:T(8,128)(2,1)S(1)}, u32[]{:S(2)}) copy-start(bf16[32,384]{1,0:T(8,128)(2,1)S(1)} %fusion.26) | copy-start | bytes 73732
  410.4 27.5 %copy-start.6 = (bf16[1,64,128,128]{3,2,1,0:T(8,128)(2,1)}, bf16[1,64,128,128]{3,2,1,0:T(8,128)(2,1)S(1)}, u32[]{:S(2)}) copy-start(bf16[1,64,128,128]{3,2,1,0:T(8,128)(2,1)S(1)} %get-tuple-element.452) | copy-start | bytes 6291460 | tf_op jit(solution)/shard_map/while
  415.8 14.7 %copy-start.1 = (f32[8192,128]{1,0:T(8,128)}, f32[8192,128]{1,0:T(8,128)S(1)}, u32[]{:S(2)}) copy-start(f32[8192,128]{1,0:T(8,128)S(1)} %get-tuple-element.454) | copy-start | bytes 12582916 | tf_op jit(solution)/shard_map/while
  437.9 3.2 copy-start.8
  441.1 22.8 %copy-start.2 = (f32[8192,128]{1,0:T(8,128)S(1)}, f32[8192,128]{1,0:T(8,128)}, u32[]{:S(2)}) copy-start(f32[8192,128]{1,0:T(8,128)} %copy-done.1) | copy-start | bytes 12582916 | tf_op jit(solution)/shard_map/while
  441.1 22.8 %copy-start.10 = (bf16[128,1024]{1,0:T(8,128)(2,1)S(1)}, bf16[128,1024]{1,0:T(8,128)(2,1)}, u32[]{:S(2)}) copy-start(bf16[128,1024]{1,0:T(8,128)(2,1)} %get-tuple-element.526) | copy-start | bytes 786436 | tf_op jit(solution)/shard_map/while
  463.9 13.3 %copy-start.5 = (f32[8192,128]{1,0:T(8,128)S(1)}, f32[8192,128]{1,0:T(8,128)}, u32[]{:S(2)}) copy-start(f32[8192,128]{1,0:T(8,128)} %fusion.156) | copy-start | bytes 12582916 | tf_op jit(solution)/shard_map/while
  482.2 3.1 copy-start.7
  496.6 7.8 copy-start.3
  496.6 7.8 copy-start.26
  516.9 6.9 copy-start.27
  519.6 4.9 copy-start.15
  527.0 27.5 %copy-start.6 = (bf16[1,64,128,128]{3,2,1,0:T(8,128)(2,1)}, bf16[1,64,128,128]{3,2,1,0:T(8,128)(2,1)S(1)}, u32[]{:S(2)}) copy-start(bf16[1,64,128,128]{3,2,1,0:T(8,128)(2,1)S(1)} %get-tuple-element.452) | copy-start | bytes 6291460 | tf_op jit(solution)/shard_map/while
  532.3 14.7 %copy-start.1 = (f32[8192,128]{1,0:T(8,128)}, f32[8192,128]{1,0:T(8,128)S(1)}, u32[]{:S(2)}) copy-start(f32[8192,128]{1,0:T(8,128)S(1)} %get-tuple-element.454) | copy-start | bytes 12582916 | tf_op jit(solution)/shard_map/while
  554.4 3.2 copy-start.8
  557.7 22.8 %copy-start.2 = (f32[8192,128]{1,0:T(8,128)S(1)}, f32[8192,128]{1,0:T(8,128)}, u32[]{:S(2)}) copy-start(f32[8192,128]{1,0:T(8,128)} %copy-done.1) | copy-start | bytes 12582916 | tf_op jit(solution)/shard_map/while
  557.7 22.8 %copy-start.10 = (bf16[128,1024]{1,0:T(8,128)(2,1)S(1)}, bf16[128,1024]{1,0:T(8,128)(2,1)}, u32[]{:S(2)}) copy-start(bf16[128,1024]{1,0:T(8,128)(2,1)} %get-tuple-element.526) | copy-start | bytes 786436 | tf_op jit(solution)/shard_map/while
  580.5 13.3 %copy-start.5 = (f32[8192,128]{1,0:T(8,128)S(1)}, f32[8192,128]{1,0:T(8,128)}, u32[]{:S(2)}) copy-start(f32[8192,128]{1,0:T(8,128)} %fusion.156) | copy-start | bytes 12582916 | tf_op jit(solution)/shard_map/while
  598.8 2.8 copy-start.4
  598.8 3.1 copy-start.7
  613.1 7.8 copy-start.3
  613.1 7.8 copy-start.26
  633.4 6.9 copy-start.27
  636.1 4.9 copy-start.15
  643.5 27.5 %copy-start.6 = (bf16[1,64,128,128]{3,2,1,0:T(8,128)(2,1)}, bf16[1,64,128,128]{3,2,1,0:T(8,128)(2,1)S(1)}, u32[]{:S(2)}) copy-start(bf16[1,64,128,128]{3,2,1,0:T(8,128)(2,1)S(1)} %get-tuple-element.452) | copy-start | bytes 6291460 | tf_op jit(solution)/shard_map/while
  648.9 14.7 %copy-start.1 = (f32[8192,128]{1,0:T(8,128)}, f32[8192,128]{1,0:T(8,128)S(1)}, u32[]{:S(2)}) copy-start(f32[8192,128]{1,0:T(8,128)S(1)} %get-tuple-element.454) | copy-start | bytes 12582916 | tf_op jit(solution)/shard_map/while
  671.0 3.2 copy-start.8
  674.2 22.8 %copy-start.2 = (f32[8192,128]{1,0:T(8,128)S(1)}, f32[8192,128]{1,0:T(8,128)}, u32[]{:S(2)}) copy-start(f32[8192,128]{1,0:T(8,128)} %copy-done.1) | copy-start | bytes 12582916 | tf_op jit(solution)/shard_map/while
  674.2 22.8 %copy-start.10 = (bf16[128,1024]{1,0:T(8,128)(2,1)S(1)}, bf16[128,1024]{1,0:T(8,128)(2,1)}, u32[]{:S(2)}) copy-start(bf16[128,1024]{1,0:T(8,128)(2,1)} %get-tuple-element.526) | copy-start | bytes 786436 | tf_op jit(solution)/shard_map/while
  697.0 13.3 %copy-start.5 = (f32[8192,128]{1,0:T(8,128)S(1)}, f32[8192,128]{1,0:T(8,128)}, u32[]{:S(2)}) copy-start(f32[8192,128]{1,0:T(8,128)} %fusion.156) | copy-start | bytes 12582916 | tf_op jit(solution)/shard_map/while
  715.3 3.1 copy-start.7
  729.6 7.8 copy-start.3
  729.6 7.8 copy-start.26
  750.0 6.9 copy-start.27
  752.7 4.9 copy-start.15
  760.1 27.5 %copy-start.6 = (bf16[1,64,128,128]{3,2,1,0:T(8,128)(2,1)}, bf16[1,64,128,128]{3,2,1,0:T(8,128)(2,1)S(1)}, u32[]{:S(2)}) copy-start(bf16[1,64,128,128]{3,2,1,0:T(8,128)(2,1)S(1)} %get-tuple-element.452) | copy-start | bytes 6291460 | tf_op jit(solution)/shard_map/while
  765.4 14.7 %copy-start.1 = (f32[8192,128]{1,0:T(8,128)}, f32[8192,128]{1,0:T(8,128)S(1)}, u32[]{:S(2)}) copy-start(f32[8192,128]{1,0:T(8,128)S(1)} %get-tuple-element.454) | copy-start | bytes 12582916 | tf_op jit(solution)/shard_map/while
  787.5 3.2 copy-start.8
  790.8 22.8 %copy-start.2 = (f32[8192,128]{1,0:T(8,128)S(1)}, f32[8192,128]{1,0:T(8,128)}, u32[]{:S(2)}) copy-start(f32[8192,128]{1,0:T(8,128)} %copy-done.1) | copy-start | bytes 12582916 | tf_op jit(solution)/shard_map/while
  790.8 22.8 %copy-start.10 = (bf16[128,1024]{1,0:T(8,128)(2,1)S(1)}, bf16[128,1024]{1,0:T(8,128)(2,1)}, u32[]{:S(2)}) copy-start(bf16[128,1024]{1,0:T(8,128)(2,1)} %get-tuple-element.526) | copy-start | bytes 786436 | tf_op jit(solution)/shard_map/while
  813.5 13.3 %copy-start.5 = (f32[8192,128]{1,0:T(8,128)S(1)}, f32[8192,128]{1,0:T(8,128)}, u32[]{:S(2)}) copy-start(f32[8192,128]{1,0:T(8,128)} %fusion.156) | copy-start | bytes 12582916 | tf_op jit(solution)/shard_map/while
  831.9 3.1 copy-start.7
  846.2 7.8 copy-start.3
  846.2 7.8 copy-start.26
  866.5 6.9 copy-start.27
  869.2 4.9 copy-start.15
  874.1 62.7 %copy-start.17 = (bf16[32,384]{1,0:T(8,128)(2,1)S(1)}, bf16[32,384]{1,0:T(8,128)(2,1)}, u32[]{:S(2)}) copy-start(bf16[32,384]{1,0:T(8,128)(2,1)} %param.20) | copy-start | bytes 73732
  874.1 62.7 %copy-start.35 = (f32[32]{0:T(128)S(1)}, f32[32]{0:T(128)}, u32[]{:S(2)}) copy-start(f32[32]{0:T(128)} %copy-done.34) | copy-start | bytes 388
  903.1 218.1 %all-reduce.3.cloned.1.call-start = ((), (), s32[]{:S(2)}) async-start(), calls=%async_computation.5 | async-start | bytes 16646144 | tf_op jit(solution)/shard_map/psum | solution.py:259
  937.9 3.5 copy-start.25
  937.9 3.4 copy-start.33
  942.3 41.4 %copy-start.12 = (bf16[384,1536]{1,0:T(8,128)(2,1)S(1)}, bf16[384,1536]{1,0:T(8,128)(2,1)}, u32[]{:S(2)}) copy-start(bf16[384,1536]{1,0:T(8,128)(2,1)} %param.29) | copy-start | bytes 3538948
  (29 other events, 57.1 us)
Sparse Core Ops, SparseCore 0:
  903.2 28.1 reduce-scatter.1
  942.4 178.8 all-reduce.2
